TPU v7x, 32 devices: a whole 2x2x4 slice. The times are simulated.
32 devices in a mesh: cells: 4 (over x, core), modes: 8 (over z, y).
Axes of the slice: x: 2, y: 2, z: 4, core: 2. Of those that a mesh axis runs over, the one named last changes fastest.
Arguments:
- hermite_coefficient_array: float32 [8, 64, 32, 2048], P('cells', None, None, 'modes'), may hold values from -6 to 6
- encounter_kernel_array: bfloat16 [14400, 120], replicated, may hold values from -0.046875 to 0.046875
- obstacle_indicator: int32 [8, 64, 32], P('cells'), may hold values 0 or 1
Outputs:
- moments_next: float32 [8, 64, 32, 2048], P('cells', None, None, 'modes')
All inputs are finite; a program needn't handle non-finite values. No bound on the sum of `obstacle_indicator` on one device may be relied on, other than what follows from the above.
Results may differ from a plain program's by a relative error of at most 0.0003.
Values sent between devices are 32-bit elements; how exact they have to be, the bound alone decides.
A program may use at most 128 MiB of HBM per device.

v0:
```python
import functools
import math

import jax
import jax.numpy as jnp
import numpy as np
from jax import lax
from jax.experimental import pallas as pl
from jax.experimental.pallas import tpu as pltpu
from jax.sharding import PartitionSpec as P

MA = 16
MB = 16
MC = 8
LDEG = 7
BASIS_SIZE = 120
MODES = 2048
BLOCK = MB * MC
WIDE = 128
GROUP = 16

CFL = 0.04
DTC = 0.2
MESH = pl.DeviceIdType.MESH


def pieces_of(edges, half):
    marks = sorted(set(edges) | {2, half + 2})
    return [(lo, hi) for lo, hi in zip(marks[:-1], marks[1:])]


def split3(x):
    hi = x.astype(jnp.bfloat16)
    rest = x - hi.astype(jnp.float32)
    mid = rest.astype(jnp.bfloat16)
    low = (rest - mid.astype(jnp.float32)).astype(jnp.bfloat16)
    return hi, mid, low


def dot(a, b):
    return jnp.dot(a, b, preferred_element_type=jnp.float32)


def kernel(cfg, hin, mask, coef, sel, sel_t, raw, out, f0, f1, tr, xh1, xh2, zh1, zh2, de1, de2,
           lx, lr, rx, rr, table, lt, rt, raw_sem, loc_sem, swap_s, swap_r, x1_s, x1_r, x2_s, x2_r, z1_s, z1_r, z2_s, z2_r,
           low_s, low_r, rate_s, rate_r, back_s, back_r, keep_sem):
    planes, rows_y, rows_z, local, nc, nm, ns, chunks = cfg
    per = local // BLOCK
    levels = 2 * per
    half = rows_y // 2
    nq = nm // 2
    size = half // chunks
    b2 = [2 + size * k for k in range(chunks + 1)]
    b1 = [1] + [b + 1 for b in b2[1:]]
    b0 = [0] + [b + 2 for b in b2[1:]]
    part = size // ns

    c = lax.axis_index("cells")
    m = lax.axis_index("modes")
    p = lax.rem(m, 2)
    q = lax.div(m, 2)
    other = 1 - p
    mate = (c, q * 2 + other)
    before = (lax.rem(c + nc - 1, nc), m)
    after = (lax.rem(c + 1, nc), m)
    below = (c, m - 2)
    above = (c, m + 2)
    has_below = q > 0
    has_above = q < nq - 1
    is_source = q < ns

    def peer(d):
        return (c, lax.rem(q + d, ns) * 2 + p)

    barrier = pltpu.get_barrier_semaphore()

    def greet(dev):
        pl.semaphore_signal(barrier, inc=1, device_id=dev, device_id_type=MESH)

    for dev in (mate, before, after):
        greet(dev)

    @pl.when(has_below)
    def _():
        greet(below)

    @pl.when(has_above)
    def _():
        greet(above)

    @pl.when(is_source)
    def _():
        for d in range(1, ns):
            greet(peer(d))

    greeted = 3 + has_below.astype(jnp.int32) + has_above.astype(jnp.int32)
    pl.semaphore_wait(barrier, greeted + (ns - 1) * is_source.astype(jnp.int32))

    def remote(src, dst, s, r, dev):
        return pltpu.make_async_remote_copy(
            src_ref=src, dst_ref=dst, send_sem=s, recv_sem=r, device_id=dev, device_id_type=MESH
        )

    pieces = pieces_of(b0, half)

    def grid_row(side, e):
        return lax.rem(side * half + (rows_y - 2) + e, rows_y)

    def swap(i):
        lo, hi = pieces[i]
        return remote(
            hin.at[:, pl.ds(grid_row(other, lo), hi - lo)],
            f0.at[p, :, pl.ds(lo, hi - lo)],
            swap_s.at[i], swap_r.at[i], mate,
        )

    def swap_in(i):
        lo, hi = pieces[i]
        return remote(
            hin.at[:, pl.ds(grid_row(other, lo), hi - lo)],
            f0.at[other, :, pl.ds(lo, hi - lo)],
            swap_s.at[i], swap_r.at[i], mate,
        )

    def own(i):
        lo, hi = pieces[i]
        return pltpu.make_async_copy(
            hin.at[:, pl.ds(grid_row(p, lo), hi - lo)],
            f0.at[p, :, pl.ds(lo, hi - lo)],
            loc_sem.at[i],
        )

    def edge(field, halo, ss, rs, blk, k, slot, bounds):
        n = bounds[k + 1] - bounds[k]
        where = pl.ds(bounds[k], n)
        up = remote(field.at[blk, planes - 1, where], halo.at[0, blk, where],
                    ss.at[0, slot, k], rs.at[0, slot, k], after)
        down = remote(field.at[blk, 0, where], halo.at[1, blk, where],
                      ss.at[1, slot, k], rs.at[1, slot, k], before)
        return up, down

    def lanes(j):
        return pl.ds((j % per) * BLOCK, BLOCK)

    def gradient(field, halo, pln, e, j):
        blk = j // per
        nxt = halo[1, blk, e, :, lanes(j)] if pln == planes - 1 else field[blk, pln + 1, e, :, lanes(j)]
        prv = halo[0, blk, e, :, lanes(j)] if pln == 0 else field[blk, pln - 1, e, :, lanes(j)]
        return nxt, prv

    def slopes(field, halo, de, lo, hi):
        def row(e, carry):
            for pln in range(planes):
                nxt, prv = gradient(field, halo, pln, e, 0)
                de[0, pln, e] = nxt - prv
                nxt, prv = gradient(field, halo, pln, e, levels - 1)
                de[1, pln, e] = nxt - prv
            return carry

        lax.fori_loop(lo, hi, row, 0)

    def to_below(de, zh, ss, rs, k, bounds):
        where = pl.ds(bounds[k], bounds[k + 1] - bounds[k])
        return remote(de.at[0, :, where], zh.at[1, :, where], ss.at[0, k], rs.at[0, k], below)

    def to_above(de, zh, ss, rs, k, bounds):
        where = pl.ds(bounds[k], bounds[k + 1] - bounds[k])
        return remote(de.at[1, :, where], zh.at[0, :, where], ss.at[1, k], rs.at[1, k], above)

    def z_start(*a):
        @pl.when(has_below)
        def _():
            to_below(*a).start()

        @pl.when(has_above)
        def _():
            to_above(*a).start()

    def z_arrived(*a):
        @pl.when(has_below)
        def _():
            to_above(*a).wait_recv()

        @pl.when(has_above)
        def _():
            to_below(*a).wait_recv()

    def z_sent(*a):
        @pl.when(has_below)
        def _():
            to_below(*a).wait_send()

        @pl.when(has_above)
        def _():
            to_above(*a).wait_send()

    wx = 0.5 * 2.0 * math.sqrt(MA)
    wy = 0.5 * 2.0 * math.sqrt(MB)
    wz = 0.5 * 2.0 * math.sqrt(MC)
    wc = 2.0 * (wx + wy + wz)

    def substep(field, halo, zh, dest, lo, hi):
        def row(e, carry):
            for pln in range(planes):
                gas = mask[pln, e]
                pairs = [gradient(field, halo, pln, e, j) for j in range(levels)]
                grads = [zh[0, pln, e]] + [a - b for a, b in pairs] + [zh[1, pln, e]]
                for j in range(levels):
                    blk = j // per
                    mid = field[blk, pln, e, :, lanes(j)]
                    ny = field[blk, pln, e + 1, :, lanes(j)]
                    py = field[blk, pln, e - 1, :, lanes(j)]
                    nz = pltpu.roll(mid, rows_z - 1, 0)
                    pz = pltpu.roll(mid, 1, 0)
                    dy = ny - py
                    dz = nz - pz
                    acc = coef[4 + j : 5 + j, :] * grads[j]
                    acc += coef[4 + levels + j : 5 + levels + j, :] * grads[j + 2]
                    acc += coef[0:1, :] * pltpu.roll(dy, MC, 1)
                    acc += coef[1:2, :] * pltpu.roll(dy, BLOCK - MC, 1)
                    acc += coef[2:3, :] * pltpu.roll(dz, 1, 1)
                    acc += coef[3:4, :] * pltpu.roll(dz, BLOCK - 1, 1)
                    acc += wx * (pairs[j][0] + pairs[j][1]) + wy * (ny + py) + wz * (nz + pz) - wc * mid
                    dest[blk, pln, e, :, lanes(j)] = mid + gas * acc
            return carry

        lax.fori_loop(lo, hi, row, 0)

    def take_low(k):
        for t in range(ns):
            lo = b2[k] + t * part
            for pln in range(planes):
                total = jnp.zeros((part * rows_z, WIDE), jnp.float32)
                for j in range(levels):
                    x = tr[j // per, pln, lo : lo + part, :, lanes(j)].reshape(part * rows_z, BLOCK)
                    for term in split3(x):
                        total += dot(term, sel[j])
                lx[k, t, pln * part * rows_z : (pln + 1) * part * rows_z] = total

    def low_copy(k, d):
        return remote(lx.at[k, lax.rem(q + d, ns)], lr.at[k, d - 1],
                      low_s.at[k, d - 1], low_r.at[k, d - 1], peer(d))

    def rate_copy(k, d):
        return remote(rx.at[k], rr.at[k, d - 1], rate_s.at[k, d - 1], rate_r.at[k, d - 1], peer(d))

    def collide(k):
        low = lx[k, q]
        for d in range(1, ns):
            low = low + lr[k, d - 1]
        lt[...] = low.T
        rt[...] = jnp.zeros_like(rt)

        def step(first, count, columns):
            rows = lt[pl.ds(first, count), :]
            values = lt[0:BASIS_SIZE, :]
            factors = jnp.concatenate(
                [(rows[i : i + 1, :] * values) for i in range(count)], axis=0
            ).astype(jnp.bfloat16)
            rt[0:BASIS_SIZE, :] += dot(table[:, columns], factors)

        def whole(g, carry):
            width = GROUP * BASIS_SIZE
            step(pl.multiple_of(g * GROUP, GROUP), GROUP, pl.ds(pl.multiple_of(g * width, WIDE), width))
            return carry

        groups = BASIS_SIZE // GROUP
        lax.fori_loop(0, groups, whole, 0)
        if groups * GROUP < BASIS_SIZE:
            step(groups * GROUP, BASIS_SIZE - groups * GROUP,
                 pl.ds(groups * GROUP * BASIS_SIZE, (BASIS_SIZE - groups * GROUP) * BASIS_SIZE))
        rx[k] = rt[...].T

    def lift(k, rates, t):
        lo = b2[k] + t * part
        terms = split3(rates)
        for j in range(levels):
            add = sum(dot(term, sel_t[j]) for term in terms) * DTC
            for pln in range(planes):
                one = add[pln * part * rows_z : (pln + 1) * part * rows_z]
                tr[j // per, pln, pl.ds(lo, part), :, lanes(j)] += one.reshape(part, rows_z, BLOCK)

    def give_back(k):
        return remote(
            tr.at[other, :, pl.ds(b2[k], size)],
            out.at[:, pl.ds(p * half + k * size, size)],
            back_s.at[k], back_r.at[k], mate,
        )

    def got_back(k):
        return remote(
            tr.at[other, :, pl.ds(b2[k], size)],
            out.at[:, pl.ds(other * half + k * size, size)],
            back_s.at[k], back_r.at[k], mate,
        )

    def keep(k):
        return pltpu.make_async_copy(
            tr.at[p, :, pl.ds(b2[k], size)],
            out.at[:, pl.ds(p * half + k * size, size)],
            keep_sem.at[k],
        )

    def finish(k):
        give_back(k).start()
        keep(k).start()

    def chunk_pieces(k):
        return [i for i, (lo, hi) in enumerate(pieces) if b0[k] <= lo and hi <= b0[k + 1]]

    ahead = 2
    lead = min(4, chunks)
    for k in range(min(ahead, chunks)):
        for i in chunk_pieces(k):
            swap(i).start()
    for i in range(len(pieces)):
        own(i).start()
    raw_copy = pltpu.make_async_copy(raw, table, raw_sem)

    @pl.when(is_source)
    def _():
        raw_copy.start()

    @pl.when(q == 0)
    def _():
        for zh in (zh1, zh2):
            zh[0] = jnp.zeros_like(zh[0])

    @pl.when(q == nq - 1)
    def _():
        for zh in (zh1, zh2):
            zh[1] = jnp.zeros_like(zh[1])

    for i in range(len(pieces)):
        own(i).wait()
    for k in range(lead):
        for copy in edge(f0, xh1, x1_s, x1_r, p, k, 0, b1):
            copy.start()

    @pl.when(is_source)
    def _():
        raw_copy.wait()

    for t in range(chunks + 7):
        if t < chunks:
            for i in chunk_pieces(t):
                swap_in(i).wait_recv()
            if t + ahead < chunks:
                for i in chunk_pieces(t + ahead):
                    swap(i).start()
            for copy in edge(f0, xh1, x1_s, x1_r, other, t, 1, b1):
                copy.start()
            if t + lead < chunks:
                for copy in edge(f0, xh1, x1_s, x1_r, p, t + lead, 0, b1):
                    copy.start()
        if 0 <= t - 1 < chunks:
            i = t - 1
            for slot, blk in enumerate((p, other)):
                for copy in edge(f0, xh1, x1_s, x1_r, blk, i, slot, b1):
                    copy.wait_recv()
            slopes(f0, xh1, de1, b1[i], b1[i + 1])
            z_start(de1, zh1, z1_s, z1_r, i, b1)
        if 0 <= t - 2 < chunks:
            i = t - 2
            z_arrived(de1, zh1, z1_s, z1_r, i, b1)
            substep(f0, xh1, zh1, f1, b1[i], b1[i + 1])
            for blk in range(2):
                for copy in edge(f1, xh2, x2_s, x2_r, blk, i, blk, b2):
                    copy.start()
        if 0 <= t - 3 < chunks:
            i = t - 3
            for blk in range(2):
                for copy in edge(f1, xh2, x2_s, x2_r, blk, i, blk, b2):
                    copy.wait_recv()
            slopes(f1, xh2, de2, b2[i], b2[i + 1])
            z_start(de2, zh2, z2_s, z2_r, i, b2)
        if 0 <= t - 4 < chunks:
            i = t - 4
            z_arrived(de2, zh2, z2_s, z2_r, i, b2)
            substep(f1, xh2, zh2, tr, b2[i], b2[i + 1])

            @pl.when(is_source)
            def _(i=i):
                take_low(i)
                for d in range(1, ns):
                    low_copy(i, d).start()

            @pl.when(jnp.logical_not(is_source))
            def _(i=i):
                finish(i)

        @pl.when(is_source)
        def _(t=t):
            if 0 <= t - 5 < chunks:
                i = t - 5
                for d in range(1, ns):
                    low_copy(i, d).wait_recv()
                collide(i)
                for d in range(1, ns):
                    rate_copy(i, d).start()
                lift(i, rx[i], q)
            if 0 <= t - 6 < chunks:
                i = t - 6
                for d in range(1, ns):
                    rate_copy(i, d).wait_recv()
                    lift(i, rr[i, d - 1], lax.rem(q + ns - d, ns))
                finish(i)

    for k in range(chunks):
        z_sent(de1, zh1, z1_s, z1_r, k, b1)
        z_sent(de2, zh2, z2_s, z2_r, k, b2)
        for slot, blk in enumerate((p, other)):
            for copy in edge(f0, xh1, x1_s, x1_r, blk, k, slot, b1):
                copy.wait_send()
        for blk in range(2):
            for copy in edge(f1, xh2, x2_s, x2_r, blk, k, blk, b2):
                copy.wait_send()
    for i in range(len(pieces)):
        swap(i).wait_send()

    @pl.when(is_source)
    def _():
        for k in range(chunks):
            for d in range(1, ns):
                low_copy(k, d).wait_send()
                rate_copy(k, d).wait_send()

    for k in range(chunks):
        keep(k).wait()
        give_back(k).wait_send()
        got_back(k).wait_recv()


def body(hermite_coefficient_array, encounter_kernel_array, obstacle_indicator):
    planes, rows_y, rows_z, local = hermite_coefficient_array.shape
    nc = lax.axis_size("cells")
    nm = lax.axis_size("modes")
    per = local // BLOCK
    levels = 2 * per
    half = rows_y // 2
    ns = -(-(LDEG + 1) // levels)
    chunks = 8
    size = half // chunks
    part = size // ns
    ext = half + 4
    m = lax.axis_index("modes")
    first_a = (m // 2) * levels

    gas = jnp.where(obstacle_indicator != 0, 0.0, CFL).astype(jnp.float32)
    gas = jnp.concatenate([gas[:, -2:], gas, gas[:, :2]], axis=1)
    gas = lax.dynamic_slice_in_dim(gas, (m % 2) * half, ext, axis=1)
    mask = jnp.broadcast_to(gas[..., None], (planes, ext, rows_z, BLOCK))

    lane = jnp.arange(BLOCK, dtype=jnp.int32)
    lane_b, lane_c = lane // MC, lane % MC
    level = first_a + jnp.arange(levels, dtype=jnp.int32)[:, None] + 0 * lane[None, :]

    def down(x):
        return jnp.sqrt(x.astype(jnp.float32))

    def up(x, count):
        return jnp.where(x + 1 < count, jnp.sqrt((x + 1).astype(jnp.float32)), 0.0)

    coef = -0.5 * jnp.concatenate(
        [
            jnp.stack([down(lane_b), up(lane_b, MB), down(lane_c), up(lane_c, MC)]),
            down(level),
            up(level, MA),
            jnp.zeros(((-(4 + 2 * levels)) % 8, BLOCK), jnp.float32),
        ],
        axis=0,
    )

    index = np.arange(MODES)
    flags = (index // BLOCK + index // MC % MB + index % MC <= LDEG).astype(np.int32)
    rank = jnp.asarray(np.where(flags == 1, np.cumsum(flags) - 1, -1), jnp.int32)
    mine = lax.dynamic_slice_in_dim(rank, first_a * BLOCK, levels * BLOCK).reshape(levels, BLOCK)
    wide = jnp.arange(WIDE, dtype=jnp.int32)
    sel = (mine[:, :, None] == wide[None, None, :]).astype(jnp.bfloat16)
    sel_t = (mine[:, None, :] == wide[None, :, None]).astype(jnp.bfloat16)

    b2 = [2 + size * k for k in range(chunks + 1)]
    count = len(pieces_of([0] + [b + 2 for b in b2[1:]], half))
    peers = max(ns - 1, 1)
    cells = planes * part * rows_z
    field = pltpu.VMEM((2, planes, ext, rows_z, local), jnp.float32)
    halo = pltpu.VMEM((2, 2, ext, rows_z, local), jnp.float32)
    slope = pltpu.VMEM((2, planes, ext, rows_z, BLOCK), jnp.float32)
    dma = pltpu.SemaphoreType.DMA
    cfg = (planes, rows_y, rows_z, local, nc, nm, ns, chunks)
    vmem = pl.BlockSpec(memory_space=pltpu.VMEM)
    return pl.pallas_call(
        functools.partial(kernel, cfg),
        out_shape=jax.ShapeDtypeStruct(hermite_coefficient_array.shape, jnp.float32),
        in_specs=[pl.BlockSpec(memory_space=pl.ANY)] + [vmem] * 4 + [pl.BlockSpec(memory_space=pl.ANY)],
        out_specs=pl.BlockSpec(memory_space=pl.ANY),
        scratch_shapes=[
            field, field, field, halo, halo, slope, slope, slope, slope,
            pltpu.VMEM((chunks, ns, cells, WIDE), jnp.float32),
            pltpu.VMEM((chunks, peers, cells, WIDE), jnp.float32),
            pltpu.VMEM((chunks, cells, WIDE), jnp.float32),
            pltpu.VMEM((chunks, peers, cells, WIDE), jnp.float32),
            pltpu.VMEM((BASIS_SIZE, BASIS_SIZE * BASIS_SIZE), jnp.bfloat16),
            pltpu.VMEM((WIDE, cells), jnp.float32),
            pltpu.VMEM((WIDE, cells), jnp.float32),
            dma, dma((count,)), dma((count,)), dma((count,)),
            dma((2, 2, chunks)), dma((2, 2, chunks)), dma((2, 2, chunks)), dma((2, 2, chunks)),
            dma((2, chunks)), dma((2, chunks)), dma((2, chunks)), dma((2, chunks)),
            dma((chunks, peers)), dma((chunks, peers)), dma((chunks, peers)), dma((chunks, peers)),
            dma((chunks,)), dma((chunks,)), dma((chunks,)),
        ],
        compiler_params=pltpu.CompilerParams(
            collective_id=0, has_side_effects=True, vmem_limit_bytes=60 * 1024 * 1024
        ),
    )(hermite_coefficient_array, mask, coef, sel, sel_t, encounter_kernel_array.T)


def solution(mesh):
    placed = (P("cells", None, None, "modes"), P(), P("cells", None, None))
    return jax.shard_map(
        body, mesh=mesh, in_specs=placed, out_specs=P("cells", None, None, "modes"), check_vma=False
    )
```

profile of v0, /device:TPU:0, one launch (start us, length us, event | category | flops | bytes accessed | tf_op | source)
XLA Modules:
  0.0 143.6 jit_solution(4284752394452078953)
XLA Ops:
  0.0 0.1 broadcast_select_fusion
  0.1 0.8 dynamic-slice_bitcast_fusion
  0.9 0.1 add.96
  1.0 0.6 broadcast_multiply_fusion.coef
  1.6 0.8 compare_select_fusion
  2.4 0.1 fusion.4
  2.5 0.1 dynamic-slice_maximum_fusion
  2.6 0.1 copy.5
  2.7 0.8 fusion.1
  3.5 1.4 broadcast_in_dim.29.mask
  4.8 133.9 %shard_map.46 = f32[2,64,32,256]{3,2,1,0:T(8,128)} custom-call(f32[2,64,32,256]{3,2,1,0:T(8,128)} %hin.1, f32[2,36,32,128]{3,2,1,0:T(8,128)} %broadcast_in_dim.29.mask, f32[16,128]{1,0:T(8,128)} %broadcast_multiply_fusion.coef, bf16[4,128,128]{2,1,0:T(8,128)(2,1)} %get-tuple-element.8.sel, bf16[4,128,128]{2,1,0:T(8,128)(2,1)} %get-tuple-element.7.sel_t, ...), custom_call_target="tpu_custom_call" | custom-call | tf_op jit(solution)/shard_map/pallas_call | solution.py:492
  138.8 4.8 %copy.7 = f32[2,64,32,256]{3,2,1,0:T(8,128)} copy(f32[2,64,32,256]{3,2,1,0:T(8,128)} %shard_map.46) | data formatting | bytes 8388608
  (6 shorter events, 0.1 us)
where the time goes:
time: 144 us
  Pallas kernels  134 us (93%)
  local copies, waits for them, and re-layouts  7.22 us (5%)
  other arithmetic  2.39 us (2%)
    pallas_call x1, Pallas kernels, body(): pl.pallas_call(functools.partial(kernel, cfg), out_shape=jax.ShapeDtypeSt...  134 us
    unnamed x1, local copies, waits for them, and re-layouts  4.79 us

commit v1 on v0

v1 whole, which is shorter than its diff:
```python
import functools
import math

import jax
import jax.numpy as jnp
import numpy as np
from jax import lax
from jax.experimental import pallas as pl
from jax.experimental.pallas import tpu as pltpu
from jax.sharding import PartitionSpec as P

MA = 16
MB = 16
MC = 8
LDEG = 7
BASIS_SIZE = 120
MODES = 2048
BLOCK = MB * MC
WIDE = 128
GROUP = 16
ROWS = 2
LEAD = 5

CFL = 0.04
DTC = 0.2
MESH = pl.DeviceIdType.MESH


def split3(x):
    hi = x.astype(jnp.bfloat16)
    rest = x - hi.astype(jnp.float32)
    mid = rest.astype(jnp.bfloat16)
    low = (rest - mid.astype(jnp.float32)).astype(jnp.bfloat16)
    return hi, mid, low


def dot(a, b):
    return jnp.dot(a, b, preferred_element_type=jnp.float32)


def loop(lo, hi, f):
    def step(i, carry):
        f(i)
        return carry

    lax.fori_loop(lo, hi, step, 0)


def kernel(cfg, hin, solid, rank, raw, out, f0, f1, tr, xh1, xh2, zh1, zh2, de1, de2,
           mask, coef, sel, sel_t, lx, lr, rx, rr, table, lt, rt, raw_sem, loc_sem, swap_s, swap_r,
           x1_s, x1_r, x2_s, x2_r, z1_s, z1_r, z2_s, z2_r, low_s, low_r, rate_s, rate_r, back_s, back_r, keep_sem):
    planes, rows_y, rows_z, local, nc, nm, ns = cfg
    per = local // BLOCK
    levels = 2 * per
    half = rows_y // 2
    ext = half + 4
    nq = nm // 2
    chunks = half // ROWS
    cells = planes * ROWS * rows_z

    c = lax.axis_index("cells")
    m = lax.axis_index("modes")
    p = lax.rem(m, 2)
    q = lax.div(m, 2)
    other = 1 - p
    mate = (c, q * 2 + other)
    before = (lax.rem(c + nc - 1, nc), m)
    after = (lax.rem(c + 1, nc), m)
    below = (c, m - 2)
    above = (c, m + 2)
    has_below = q > 0
    has_above = q < nq - 1
    is_source = q < ns

    def peer(d):
        return (c, lax.rem(q + d, ns) * 2 + p)

    barrier = pltpu.get_barrier_semaphore()

    def greet(dev):
        pl.semaphore_signal(barrier, inc=1, device_id=dev, device_id_type=MESH)

    for dev in (mate, before, after):
        greet(dev)

    @pl.when(has_below)
    def _():
        greet(below)

    @pl.when(has_above)
    def _():
        greet(above)

    @pl.when(is_source)
    def _():
        for d in range(1, ns):
            greet(peer(d))

    def grid_row(side, e):
        return lax.rem(side * half + (rows_y - 2) + e, rows_y)

    own_pieces = [(0, 2), (2, half + 2), (half + 2, ext)]

    def own(i):
        lo, hi = own_pieces[i]
        return pltpu.make_async_copy(
            hin.at[:, pl.ds(grid_row(p, lo), hi - lo)],
            f0.at[p, :, pl.ds(lo, hi - lo)],
            loc_sem.at[i],
        )

    for i in range(len(own_pieces)):
        own(i).start()
    raw_copy = pltpu.make_async_copy(raw, table, raw_sem)

    greeted = 3 + has_below.astype(jnp.int32) + has_above.astype(jnp.int32)
    pl.semaphore_wait(barrier, greeted + (ns - 1) * is_source.astype(jnp.int32))

    def remote(src, dst, s, r, dev):
        return pltpu.make_async_remote_copy(
            src_ref=src, dst_ref=dst, send_sem=s, recv_sem=r, device_id=dev, device_id_type=MESH
        )

    arrivals = ext // ROWS
    first = chunks + 1

    def rows0(k):
        return pl.ds(k * ROWS, ROWS)

    def rows1(i):
        return pl.ds(i * ROWS + 1, ROWS)

    def rows2(j):
        return pl.ds(j * ROWS + 2, ROWS)

    def swap(k):
        where = pl.ds(grid_row(other, k * ROWS), ROWS)
        return remote(hin.at[:, where], f0.at[p, :, rows0(k)], swap_s.at[k], swap_r.at[k], mate)

    def swap_in(k):
        where = pl.ds(grid_row(other, k * ROWS), ROWS)
        return remote(hin.at[:, where], f0.at[other, :, rows0(k)], swap_s.at[k], swap_r.at[k], mate)

    def edge(field, halo, ss, rs, blk, k, slot, where):
        up = remote(field.at[blk, planes - 1, where], halo.at[0, blk, where],
                    ss.at[0, slot, k], rs.at[0, slot, k], after)
        down = remote(field.at[blk, 0, where], halo.at[1, blk, where],
                      ss.at[1, slot, k], rs.at[1, slot, k], before)
        return up, down

    def edge1(slot, i):
        return edge(f0, xh1, x1_s, x1_r, (p, other)[slot], i, slot, rows1(i))

    def edge2(blk, j):
        return edge(f1, xh2, x2_s, x2_r, blk, j, blk, rows2(j))

    def lanes(j):
        return pl.ds((j % per) * BLOCK, BLOCK)

    def gradient(field, halo, pln, e, j):
        blk = j // per
        nxt = halo[1, blk, e, :, lanes(j)] if pln == planes - 1 else field[blk, pln + 1, e, :, lanes(j)]
        prv = halo[0, blk, e, :, lanes(j)] if pln == 0 else field[blk, pln - 1, e, :, lanes(j)]
        return nxt, prv

    def slopes(field, halo, de, lo):
        def row(r):
            e = lo + r
            for pln in range(planes):
                nxt, prv = gradient(field, halo, pln, e, 0)
                de[0, pln, e] = nxt - prv
                nxt, prv = gradient(field, halo, pln, e, levels - 1)
                de[1, pln, e] = nxt - prv

        loop(0, ROWS, row)

    def to_below(de, zh, ss, rs, k, where):
        return remote(de.at[0, :, where], zh.at[1, :, where], ss.at[0, k], rs.at[0, k], below)

    def to_above(de, zh, ss, rs, k, where):
        return remote(de.at[1, :, where], zh.at[0, :, where], ss.at[1, k], rs.at[1, k], above)

    def z_start(*a):
        @pl.when(has_below)
        def _():
            to_below(*a).start()

        @pl.when(has_above)
        def _():
            to_above(*a).start()

    def z_arrived(*a):
        @pl.when(has_below)
        def _():
            to_above(*a).wait_recv()

        @pl.when(has_above)
        def _():
            to_below(*a).wait_recv()

    def z_sent(*a):
        @pl.when(has_below)
        def _():
            to_below(*a).wait_send()

        @pl.when(has_above)
        def _():
            to_above(*a).wait_send()

    def z1(i):
        return de1, zh1, z1_s, z1_r, i, rows1(i)

    def z2(j):
        return de2, zh2, z2_s, z2_r, j, rows2(j)

    wx = 0.5 * 2.0 * math.sqrt(MA)
    wy = 0.5 * 2.0 * math.sqrt(MB)
    wz = 0.5 * 2.0 * math.sqrt(MC)
    wc = 2.0 * (wx + wy + wz)

    def substep(field, halo, zh, dest, lo):
        def row(r):
            e = lo + r
            for pln in range(planes):
                gas = mask[pln, e]
                pairs = [gradient(field, halo, pln, e, j) for j in range(levels)]
                grads = [zh[0, pln, e]] + [a - b for a, b in pairs] + [zh[1, pln, e]]
                for j in range(levels):
                    blk = j // per
                    mid = field[blk, pln, e, :, lanes(j)]
                    ny = field[blk, pln, e + 1, :, lanes(j)]
                    py = field[blk, pln, e - 1, :, lanes(j)]
                    nz = pltpu.roll(mid, rows_z - 1, 0)
                    pz = pltpu.roll(mid, 1, 0)
                    dy = ny - py
                    dz = nz - pz
                    acc = coef[4 + j : 5 + j, :] * grads[j]
                    acc += coef[4 + levels + j : 5 + levels + j, :] * grads[j + 2]
                    acc += coef[0:1, :] * pltpu.roll(dy, MC, 1)
                    acc += coef[1:2, :] * pltpu.roll(dy, BLOCK - MC, 1)
                    acc += coef[2:3, :] * pltpu.roll(dz, 1, 1)
                    acc += coef[3:4, :] * pltpu.roll(dz, BLOCK - 1, 1)
                    acc += wx * (pairs[j][0] + pairs[j][1]) + wy * (ny + py) + wz * (nz + pz) - wc * mid
                    dest[blk, pln, e, :, lanes(j)] = mid + gas * acc

        loop(0, ROWS, row)

    def take_low(j):
        total = jnp.zeros((cells, WIDE), jnp.float32)
        for level in range(levels):
            x = tr[level // per, :, rows2(j), :, lanes(level)].reshape(cells, BLOCK)
            for term in split3(x):
                total += dot(term, sel[level])
        lx[j] = total

    def owner(j):
        return lax.rem(j, ns)

    def distance(j):
        return lax.rem(owner(j) + ns - q, ns)

    def low_send(j):
        return remote(lx.at[j], lr.at[j, distance(j) - 1], low_s.at[j], low_r.at[j, distance(j) - 1],
                      (c, owner(j) * 2 + p))

    def low_take(j, d):
        return remote(lx.at[j], lr.at[j, d - 1], low_s.at[j], low_r.at[j, d - 1], peer(d))

    def rate_send(j, d):
        return remote(rx.at[j], rr.at[j], rate_s.at[j, d - 1], rate_r.at[j], peer(d))

    def rate_take(j):
        return remote(rx.at[j], rr.at[j], rate_s.at[j, 0], rate_r.at[j], peer(ns - 1))

    def collide(j):
        low = lx[j]
        for d in range(1, ns):
            low = low + lr[j, d - 1]
        lt[...] = low.T
        rt[...] = jnp.zeros_like(rt)

        def step(start, count, columns):
            rows = lt[pl.ds(start, count), :]
            values = lt[0:BASIS_SIZE, :]
            factors = jnp.concatenate(
                [(rows[i : i + 1, :] * values) for i in range(count)], axis=0
            ).astype(jnp.bfloat16)
            rt[0:BASIS_SIZE, :] += dot(table[:, columns], factors)

        def whole(g):
            width = GROUP * BASIS_SIZE
            step(pl.multiple_of(g * GROUP, GROUP), GROUP, pl.ds(pl.multiple_of(g * width, WIDE), width))

        groups = BASIS_SIZE // GROUP
        loop(0, groups, whole)
        if groups * GROUP < BASIS_SIZE:
            step(groups * GROUP, BASIS_SIZE - groups * GROUP,
                 pl.ds(groups * GROUP * BASIS_SIZE, (BASIS_SIZE - groups * GROUP) * BASIS_SIZE))
        rx[j] = rt[...].T

    def lift(j, rates):
        terms = split3(rates)
        for level in range(levels):
            add = sum(dot(term, sel_t[level]) for term in terms) * DTC
            tr[level // per, :, rows2(j), :, lanes(level)] += add.reshape(planes, ROWS, rows_z, BLOCK)

    def give_back(j):
        return remote(tr.at[other, :, rows2(j)], out.at[:, pl.ds(p * half + j * ROWS, ROWS)],
                      back_s.at[j], back_r.at[j], mate)

    def got_back(j):
        return remote(tr.at[other, :, rows2(j)], out.at[:, pl.ds(other * half + j * ROWS, ROWS)],
                      back_s.at[j], back_r.at[j], mate)

    def keep(j):
        return pltpu.make_async_copy(tr.at[p, :, rows2(j)], out.at[:, pl.ds(p * half + j * ROWS, ROWS)],
                                     keep_sem.at[j])

    def finish(j):
        give_back(j).start()
        keep(j).start()

    def start_all(copies):
        for copy in copies:
            copy.start()

    def during(index, count, f):
        @pl.when(jnp.logical_and(index >= 0, index < count))
        def _():
            f(index)

    loop(0, 2, lambda k: swap(k).start())
    for i in range(len(own_pieces)):
        own(i).wait()
    loop(0, min(LEAD, first), lambda i: start_all(edge1(0, i)))
    loop(2, arrivals, lambda k: swap(k).start())

    @pl.when(is_source)
    def _():
        raw_copy.start()

    @pl.when(q == 0)
    def _():
        for zh in (zh1, zh2):
            zh[0] = jnp.zeros_like(zh[0])

    @pl.when(q == nq - 1)
    def _():
        for zh in (zh1, zh2):
            zh[1] = jnp.zeros_like(zh[1])

    lane = lax.broadcasted_iota(jnp.int32, (1, BLOCK), 1)
    lane_b, lane_c = lax.div(lane, MC), lax.rem(lane, MC)

    def low_root(x):
        return -0.5 * jnp.sqrt(x.astype(jnp.float32))

    def high_root(x, count):
        return jnp.where(x + 1 < count, -0.5 * jnp.sqrt((x + 1).astype(jnp.float32)), 0.0)

    coef[0:1] = low_root(lane_b)
    coef[1:2] = high_root(lane_b, MB)
    coef[2:3] = low_root(lane_c)
    coef[3:4] = high_root(lane_c, MC)
    wide = lax.broadcasted_iota(jnp.int32, (WIDE, BLOCK), 0)
    for j in range(levels):
        level = q * levels + j
        coef[4 + j : 5 + j] = low_root(0 * lane + level)
        coef[4 + levels + j : 5 + levels + j] = high_root(0 * lane + level, MA)
        mine = jnp.where(rank[pl.ds(level, 1), :] == wide, 1.0, 0.0)
        sel_t[j] = mine.astype(jnp.bfloat16)
        sel[j] = mine.T.astype(jnp.bfloat16)

    clear = [jnp.where(solid[pln] != 0, 0.0, 1.0).astype(jnp.bfloat16) for pln in range(planes)]
    line = lax.broadcasted_iota(jnp.int32, (rows_y, BLOCK), 0)

    def spread(e):
        pick = jnp.where(line == grid_row(p, e), 1.0, 0.0).astype(jnp.bfloat16)
        for pln in range(planes):
            mask[pln, e] = dot(clear[pln], pick) * CFL

    loop(1, ext - 1, spread)

    def advance(t):
        def arrive(i):
            @pl.when(i == 0)
            def _():
                swap_in(0).wait_recv()

            swap_in(i + 1).wait_recv()
            start_all(edge1(1, i))

            @pl.when(i + LEAD < first)
            def _():
                start_all(edge1(0, i + LEAD))

        def slope1(i):
            for slot in range(2):
                for copy in edge1(slot, i):
                    copy.wait_recv()
            slopes(f0, xh1, de1, i * ROWS + 1)
            z_start(*z1(i))

        def slope2(j):
            for blk in range(2):
                for copy in edge2(blk, j):
                    copy.wait_recv()
            slopes(f1, xh2, de2, j * ROWS + 2)
            z_start(*z2(j))

        def move1(i):
            z_arrived(*z1(i))
            substep(f0, xh1, zh1, f1, i * ROWS + 1)

            @pl.when(i >= 1)
            def _():
                for blk in range(2):
                    start_all(edge2(blk, i - 1))

        def move2(j):
            z_arrived(*z2(j))
            substep(f1, xh2, zh2, tr, j * ROWS + 2)

            @pl.when(is_source)
            def _():
                take_low(j)

                @pl.when(q != owner(j))
                def _():
                    low_send(j).start()

            @pl.when(jnp.logical_not(is_source))
            def _():
                finish(j)

        def meet(j):
            @pl.when(jnp.logical_and(is_source, q == owner(j)))
            def _():
                for d in range(1, ns):
                    low_take(j, d).wait_recv()
                collide(j)
                for d in range(1, ns):
                    rate_send(j, d).start()
                lift(j, rx[j])
                finish(j)

        def settle(j):
            @pl.when(jnp.logical_and(is_source, q != owner(j)))
            def _():
                rate_take(j).wait_recv()
                lift(j, rr[j])
                finish(j)

        during(t, first, arrive)
        during(t - 2, first, slope1)
        during(t - 6, chunks, slope2)
        during(t - 3, first, move1)
        during(t - 7, chunks, move2)

        @pl.when(jnp.logical_and(is_source, t == 8))
        def _():
            raw_copy.wait()

        during(t - 8, chunks, meet)
        during(t - 10, chunks, settle)

    loop(0, chunks + 11, advance)

    def drain1(i):
        z_sent(*z1(i))
        for slot in range(2):
            for copy in edge1(slot, i):
                copy.wait_send()

    def drain2(j):
        z_sent(*z2(j))
        for blk in range(2):
            for copy in edge2(blk, j):
                copy.wait_send()

        @pl.when(jnp.logical_and(is_source, q == owner(j)))
        def _():
            for d in range(1, ns):
                rate_send(j, d).wait_send()

        @pl.when(jnp.logical_and(is_source, q != owner(j)))
        def _():
            low_send(j).wait_send()

    loop(0, arrivals, lambda k: swap(k).wait_send())
    loop(0, first, drain1)
    loop(0, chunks, drain2)

    def drain3(j):
        keep(j).wait()
        give_back(j).wait_send()
        got_back(j).wait_recv()

    loop(0, chunks, drain3)


def body(hermite_coefficient_array, encounter_kernel_array, obstacle_indicator):
    planes, rows_y, rows_z, local = hermite_coefficient_array.shape
    nc = lax.axis_size("cells")
    nm = lax.axis_size("modes")
    per = local // BLOCK
    levels = 2 * per
    half = rows_y // 2
    ns = -(-(LDEG + 1) // levels)
    chunks = half // ROWS
    ext = half + 4

    index = np.arange(MODES)
    flags = (index // BLOCK + index // MC % MB + index % MC <= LDEG).astype(np.int32)
    rank = jnp.asarray(np.where(flags == 1, np.cumsum(flags) - 1, -1).reshape(MA, BLOCK), jnp.int32)

    peers = max(ns - 1, 1)
    cells = planes * ROWS * rows_z
    field = pltpu.VMEM((2, planes, ext, rows_z, local), jnp.float32)
    halo = pltpu.VMEM((2, 2, ext, rows_z, local), jnp.float32)
    slope = pltpu.VMEM((2, planes, ext, rows_z, BLOCK), jnp.float32)
    dma = pltpu.SemaphoreType.DMA
    cfg = (planes, rows_y, rows_z, local, nc, nm, ns)
    vmem = pl.BlockSpec(memory_space=pltpu.VMEM)
    anywhere = pl.BlockSpec(memory_space=pl.ANY)
    return pl.pallas_call(
        functools.partial(kernel, cfg),
        out_shape=pltpu.VMEM(hermite_coefficient_array.shape, jnp.float32),
        in_specs=[anywhere, vmem, vmem, anywhere],
        out_specs=vmem,
        scratch_shapes=[
            field, field, field, halo, halo, slope, slope, slope, slope,
            pltpu.VMEM((planes, ext, rows_z, BLOCK), jnp.float32),
            pltpu.VMEM((4 + 2 * levels + -(4 + 2 * levels) % 8, BLOCK), jnp.float32),
            pltpu.VMEM((levels, BLOCK, WIDE), jnp.bfloat16),
            pltpu.VMEM((levels, WIDE, BLOCK), jnp.bfloat16),
            pltpu.VMEM((chunks, cells, WIDE), jnp.float32),
            pltpu.VMEM((chunks, peers, cells, WIDE), jnp.float32),
            pltpu.VMEM((chunks, cells, WIDE), jnp.float32),
            pltpu.VMEM((chunks, cells, WIDE), jnp.float32),
            pltpu.VMEM((BASIS_SIZE, BASIS_SIZE * BASIS_SIZE), jnp.bfloat16),
            pltpu.VMEM((WIDE, cells), jnp.float32),
            pltpu.VMEM((WIDE, cells), jnp.float32),
            dma, dma((3,)), dma((ext // ROWS,)), dma((ext // ROWS,)),
            dma((2, 2, chunks + 1)), dma((2, 2, chunks + 1)), dma((2, 2, chunks)), dma((2, 2, chunks)),
            dma((2, chunks + 1)), dma((2, chunks + 1)), dma((2, chunks)), dma((2, chunks)),
            dma((chunks,)), dma((chunks, peers)), dma((chunks, peers)), dma((chunks,)),
            dma((chunks,)), dma((chunks,)), dma((chunks,)),
        ],
        compiler_params=pltpu.CompilerParams(
            collective_id=0, has_side_effects=True, vmem_limit_bytes=54 * 1024 * 1024
        ),
    )(hermite_coefficient_array, obstacle_indicator.transpose(0, 2, 1), rank, encounter_kernel_array.T)


def solution(mesh):
    placed = (P("cells", None, None, "modes"), P(), P("cells", None, None))
    return jax.shard_map(
        body, mesh=mesh, in_specs=placed, out_specs=P("cells", None, None, "modes"), check_vma=False
    )
```

time: 144 us -> 126 us (0.88)
  Pallas kernels: 134 us -> 124 us
  local copies, waits for them, and re-layouts: 7.22 us -> 2.02 us
  other arithmetic: 2.39 us -> 0 us
    pallas_call x1, Pallas kernels: 134 us -> 124 us  [body(): pl.pallas_call(functools.partial(kernel, cfg), out_shape=pltpu.VMEM(hermi...]
    unnamed x1, local copies, waits for them, and re-layouts: 4.79 us -> 2.02 us
where the time goes in v1:
time: 126 us
  Pallas kernels  124 us (98%)
  local copies, waits for them, and re-layouts  2.02 us (2%)
    pallas_call x1, Pallas kernels, body(): pl.pallas_call(functools.partial(kernel, cfg), out_shape=pltpu.VMEM(hermi...  124 us

profile of v1, /device:TPU:0, one launch (start us, length us, event | category | flops | bytes accessed | tf_op | source)
XLA Modules:
  0.0 126.0 jit_solution(4307871306039657847)
XLA Ops:
  0.0 124.0 %shard_map.46 = f32[2,64,32,256]{3,2,1,0:T(8,128)S(1)} custom-call(f32[2,64,32,256]{3,2,1,0:T(8,128)} %hin.1, s32[2,32,64]{2,1,0:T(8,128)} %bitcast.3, s32[16,128]{1,0:T(8,128)} %constant.2.clone.rank, bf16[120,14400]{1,0:T(8,128)(2,1)} %bitcast.2), custom_call_target="tpu_custom_call" | custom-call | tf_op jit(solution)/shard_map/pallas_call | solution.py:526
  124.0 2.0 %copy.6 = f32[2,64,32,256]{3,2,1,0:T(8,128)} copy(f32[2,64,32,256]{3,2,1,0:T(8,128)S(1)} %shard_map.46) | data formatting | bytes 8388608

commit v2 on v1

--- a/solution.py
+++ b/solution.py
@@ -17,7 +17,7 @@
 MODES = 2048
 BLOCK = MB * MC
 WIDE = 128
-GROUP = 16
+GROUP = 64
 ROWS = 2
 LEAD = 5
 
@@ -48,7 +48,7 @@
 
 def kernel(cfg, hin, solid, rank, raw, out, f0, f1, tr, xh1, xh2, zh1, zh2, de1, de2,
            mask, coef, sel, sel_t, lx, lr, rx, rr, table, lt, rt, raw_sem, loc_sem, swap_s, swap_r,
-           x1_s, x1_r, x2_s, x2_r, z1_s, z1_r, z2_s, z2_r, low_s, low_r, rate_s, rate_r, back_s, back_r, keep_sem):
+           x1_s, x1_r, x2_s, x2_r, z1_s, z1_r, z2_s, z2_r, low_s, rate_s, meet_r, back_s, back_r, keep_sem):
     planes, rows_y, rows_z, local, nc, nm, ns = cfg
     per = local // BLOCK
     levels = 2 * per
@@ -106,7 +106,7 @@
         return pltpu.make_async_copy(
             hin.at[:, pl.ds(grid_row(p, lo), hi - lo)],
             f0.at[p, :, pl.ds(lo, hi - lo)],
-            loc_sem.at[i],
+            loc_sem,
         )
 
     for i in range(len(own_pieces)):
@@ -135,24 +135,25 @@
 
     def swap(k):
         where = pl.ds(grid_row(other, k * ROWS), ROWS)
-        return remote(hin.at[:, where], f0.at[p, :, rows0(k)], swap_s.at[k], swap_r.at[k], mate)
+        return remote(hin.at[:, where], f0.at[p, :, rows0(k)], swap_s, swap_r.at[k], mate)
 
     def swap_in(k):
         where = pl.ds(grid_row(other, k * ROWS), ROWS)
-        return remote(hin.at[:, where], f0.at[other, :, rows0(k)], swap_s.at[k], swap_r.at[k], mate)
-
-    def edge(field, halo, ss, rs, blk, k, slot, where):
-        up = remote(field.at[blk, planes - 1, where], halo.at[0, blk, where],
-                    ss.at[0, slot, k], rs.at[0, slot, k], after)
-        down = remote(field.at[blk, 0, where], halo.at[1, blk, where],
-                      ss.at[1, slot, k], rs.at[1, slot, k], before)
+        return remote(hin.at[:, where], f0.at[other, :, rows0(k)], swap_s, swap_r.at[k], mate)
+
+    def edge(field, halo, ss, rs, blk, k, where):
+        up = remote(field.at[blk, planes - 1, where], halo.at[0, blk, where], ss, rs.at[k], after)
+        down = remote(field.at[blk, 0, where], halo.at[1, blk, where], ss, rs.at[k], before)
         return up, down
 
     def edge1(slot, i):
-        return edge(f0, xh1, x1_s, x1_r, (p, other)[slot], i, slot, rows1(i))
+        return edge(f0, xh1, x1_s, x1_r, (p, other)[slot], i, rows1(i))
 
     def edge2(blk, j):
-        return edge(f1, xh2, x2_s, x2_r, blk, j, blk, rows2(j))
+        return edge(f1, xh2, x2_s, x2_r, blk, j, rows2(j))
+
+    def whole(ref, s, r):
+        return remote(ref, ref, s, r, mate)
 
     def lanes(j):
         return pl.ds((j % per) * BLOCK, BLOCK)
@@ -175,10 +176,10 @@
         loop(0, ROWS, row)
 
     def to_below(de, zh, ss, rs, k, where):
-        return remote(de.at[0, :, where], zh.at[1, :, where], ss.at[0, k], rs.at[0, k], below)
+        return remote(de.at[0, :, where], zh.at[1, :, where], ss, rs.at[k], below)
 
     def to_above(de, zh, ss, rs, k, where):
-        return remote(de.at[1, :, where], zh.at[0, :, where], ss.at[1, k], rs.at[1, k], above)
+        return remote(de.at[1, :, where], zh.at[0, :, where], ss, rs.at[k], above)
 
     def z_start(*a):
         @pl.when(has_below)
@@ -189,23 +190,26 @@
         def _():
             to_above(*a).start()
 
-    def z_arrived(*a):
-        @pl.when(has_below)
-        def _():
-            to_above(*a).wait_recv()
-
-        @pl.when(has_above)
-        def _():
-            to_below(*a).wait_recv()
-
-    def z_sent(*a):
-        @pl.when(has_below)
-        def _():
-            to_below(*a).wait_send()
-
-        @pl.when(has_above)
-        def _():
-            to_above(*a).wait_send()
+    inner = jnp.logical_and(has_below, has_above)
+    outer = jnp.logical_xor(has_below, has_above)
+
+    def z_arrived(de, zh, ss, rs, k, where):
+        @pl.when(inner)
+        def _():
+            whole(zh.at[:, :, where], ss, rs.at[k]).wait_recv()
+
+        @pl.when(outer)
+        def _():
+            whole(zh.at[0, :, where], ss, rs.at[k]).wait_recv()
+
+    def z_sent(de, ss, where):
+        @pl.when(inner)
+        def _():
+            whole(de.at[:, :, where], ss, ss).wait_send()
+
+        @pl.when(outer)
+        def _():
+            whole(de.at[0, :, where], ss, ss).wait_send()
 
     def z1(i):
         return de1, zh1, z1_s, z1_r, i, rows1(i)
@@ -260,17 +264,10 @@
         return lax.rem(owner(j) + ns - q, ns)
 
     def low_send(j):
-        return remote(lx.at[j], lr.at[j, distance(j) - 1], low_s.at[j], low_r.at[j, distance(j) - 1],
-                      (c, owner(j) * 2 + p))
-
-    def low_take(j, d):
-        return remote(lx.at[j], lr.at[j, d - 1], low_s.at[j], low_r.at[j, d - 1], peer(d))
+        return remote(lx.at[j], lr.at[j, distance(j) - 1], low_s, meet_r.at[j], (c, owner(j) * 2 + p))
 
     def rate_send(j, d):
-        return remote(rx.at[j], rr.at[j], rate_s.at[j, d - 1], rate_r.at[j], peer(d))
-
-    def rate_take(j):
-        return remote(rx.at[j], rr.at[j], rate_s.at[j, 0], rate_r.at[j], peer(ns - 1))
+        return remote(rx.at[j], rr.at[j], rate_s, meet_r.at[j], peer(d))
 
     def collide(j):
         low = lx[j]
@@ -287,12 +284,12 @@
             ).astype(jnp.bfloat16)
             rt[0:BASIS_SIZE, :] += dot(table[:, columns], factors)
 
-        def whole(g):
+        def block(g):
             width = GROUP * BASIS_SIZE
             step(pl.multiple_of(g * GROUP, GROUP), GROUP, pl.ds(pl.multiple_of(g * width, WIDE), width))
 
         groups = BASIS_SIZE // GROUP
-        loop(0, groups, whole)
+        loop(0, groups, block)
         if groups * GROUP < BASIS_SIZE:
             step(groups * GROUP, BASIS_SIZE - groups * GROUP,
                  pl.ds(groups * GROUP * BASIS_SIZE, (BASIS_SIZE - groups * GROUP) * BASIS_SIZE))
@@ -306,15 +303,11 @@
 
     def give_back(j):
         return remote(tr.at[other, :, rows2(j)], out.at[:, pl.ds(p * half + j * ROWS, ROWS)],
-                      back_s.at[j], back_r.at[j], mate)
-
-    def got_back(j):
-        return remote(tr.at[other, :, rows2(j)], out.at[:, pl.ds(other * half + j * ROWS, ROWS)],
-                      back_s.at[j], back_r.at[j], mate)
+                      back_s, back_r, mate)
 
     def keep(j):
         return pltpu.make_async_copy(tr.at[p, :, rows2(j)], out.at[:, pl.ds(p * half + j * ROWS, ROWS)],
-                                     keep_sem.at[j])
+                                     keep_sem)
 
     def finish(j):
         give_back(j).start()
@@ -330,8 +323,7 @@
             f(index)
 
     loop(0, 2, lambda k: swap(k).start())
-    for i in range(len(own_pieces)):
-        own(i).wait()
+    pltpu.make_async_copy(f0.at[p], f0.at[p], loc_sem).wait()
     loop(0, min(LEAD, first), lambda i: start_all(edge1(0, i)))
     loop(2, arrivals, lambda k: swap(k).start())
 
@@ -395,16 +387,12 @@
                 start_all(edge1(0, i + LEAD))
 
         def slope1(i):
-            for slot in range(2):
-                for copy in edge1(slot, i):
-                    copy.wait_recv()
+            whole(xh1.at[:, :, rows1(i)], x1_s, x1_r.at[i]).wait_recv()
             slopes(f0, xh1, de1, i * ROWS + 1)
             z_start(*z1(i))
 
         def slope2(j):
-            for blk in range(2):
-                for copy in edge2(blk, j):
-                    copy.wait_recv()
+            whole(xh2.at[:, :, rows2(j)], x2_s, x2_r.at[j]).wait_recv()
             slopes(f1, xh2, de2, j * ROWS + 2)
             z_start(*z2(j))
 
@@ -436,8 +424,8 @@
         def meet(j):
             @pl.when(jnp.logical_and(is_source, q == owner(j)))
             def _():
-                for d in range(1, ns):
-                    low_take(j, d).wait_recv()
+                if ns > 1:
+                    whole(lr.at[j], low_s, meet_r.at[j]).wait_recv()
                 collide(j)
                 for d in range(1, ns):
                     rate_send(j, d).start()
@@ -447,7 +435,7 @@
         def settle(j):
             @pl.when(jnp.logical_and(is_source, q != owner(j)))
             def _():
-                rate_take(j).wait_recv()
+                whole(rr.at[j], rate_s, meet_r.at[j]).wait_recv()
                 lift(j, rr[j])
                 finish(j)
 
@@ -466,37 +454,21 @@
 
     loop(0, chunks + 11, advance)
 
-    def drain1(i):
-        z_sent(*z1(i))
-        for slot in range(2):
-            for copy in edge1(slot, i):
-                copy.wait_send()
-
-    def drain2(j):
-        z_sent(*z2(j))
-        for blk in range(2):
-            for copy in edge2(blk, j):
-                copy.wait_send()
-
-        @pl.when(jnp.logical_and(is_source, q == owner(j)))
-        def _():
-            for d in range(1, ns):
-                rate_send(j, d).wait_send()
-
-        @pl.when(jnp.logical_and(is_source, q != owner(j)))
-        def _():
-            low_send(j).wait_send()
-
-    loop(0, arrivals, lambda k: swap(k).wait_send())
-    loop(0, first, drain1)
-    loop(0, chunks, drain2)
-
-    def drain3(j):
-        keep(j).wait()
-        give_back(j).wait_send()
-        got_back(j).wait_recv()
-
-    loop(0, chunks, drain3)
+    whole(f0.at[p], swap_s, swap_s).wait_send()
+    whole(xh1.at[:, :, pl.ds(1, first * ROWS)], x1_s, x1_s).wait_send()
+    whole(xh2.at[:, :, pl.ds(2, half)], x2_s, x2_s).wait_send()
+    z_sent(de1, z1_s, pl.ds(1, first * ROWS))
+    z_sent(de2, z2_s, pl.ds(2, half))
+    if ns > 1:
+        @pl.when(is_source)
+        def _():
+            share = chunks // ns
+            whole(lx.at[pl.ds(0, chunks - share)], low_s, low_s).wait_send()
+            whole(lx.at[pl.ds(0, share * (ns - 1))], rate_s, rate_s).wait_send()
+
+    pltpu.make_async_copy(tr.at[p, :, pl.ds(2, half)], tr.at[p, :, pl.ds(2, half)], keep_sem).wait()
+    whole(tr.at[other, :, pl.ds(2, half)], back_s, back_s).wait_send()
+    whole(out.at[:, pl.ds(other * half, half)], back_r, back_r).wait_recv()
 
 
 def body(hermite_coefficient_array, encounter_kernel_array, obstacle_indicator):
@@ -541,11 +513,8 @@
             pltpu.VMEM((BASIS_SIZE, BASIS_SIZE * BASIS_SIZE), jnp.bfloat16),
             pltpu.VMEM((WIDE, cells), jnp.float32),
             pltpu.VMEM((WIDE, cells), jnp.float32),
-            dma, dma((3,)), dma((ext // ROWS,)), dma((ext // ROWS,)),
-            dma((2, 2, chunks + 1)), dma((2, 2, chunks + 1)), dma((2, 2, chunks)), dma((2, 2, chunks)),
-            dma((2, chunks + 1)), dma((2, chunks + 1)), dma((2, chunks)), dma((2, chunks)),
-            dma((chunks,)), dma((chunks, peers)), dma((chunks, peers)), dma((chunks,)),
-            dma((chunks,)), dma((chunks,)), dma((chunks,)),
+            dma, dma, dma, dma((ext // ROWS,)), dma, dma((chunks + 1,)), dma, dma((chunks,)),
+            dma, dma((chunks + 1,)), dma, dma((chunks,)), dma, dma, dma((chunks,)), dma, dma, dma,
         ],
         compiler_params=pltpu.CompilerParams(
             collective_id=0, has_side_effects=True, vmem_limit_bytes=54 * 1024 * 1024

time: 126 us -> 120 us (0.952)
  Pallas kernels: 124 us -> 118 us
    pallas_call x1, Pallas kernels: 124 us -> 118 us  [body(): pl.pallas_call(functools.partial(kernel, cfg), out_shape=pltpu.VMEM(hermi...]
where the time goes in v2:
time: 120 us
  Pallas kernels  118 us (98%)
  local copies, waits for them, and re-layouts  2.02 us (2%)
    pallas_call x1, Pallas kernels, body(): pl.pallas_call(functools.partial(kernel, cfg), out_shape=pltpu.VMEM(hermi...  118 us

profile of v2, /device:TPU:0, one launch (start us, length us, event | category | flops | bytes accessed | tf_op | source)
XLA Modules:
  0.0 119.9 jit_solution(11840493303791369867)
XLA Ops:
  0.0 117.9 %shard_map.46 = f32[2,64,32,256]{3,2,1,0:T(8,128)S(1)} custom-call(f32[2,64,32,256]{3,2,1,0:T(8,128)} %hin.1, s32[2,32,64]{2,1,0:T(8,128)} %bitcast.3, s32[16,128]{1,0:T(8,128)} %constant.2.clone.rank, bf16[120,14400]{1,0:T(8,128)(2,1)} %bitcast.2), custom_call_target="tpu_custom_call" | custom-call | tf_op jit(solution)/shard_map/pallas_call | solution.py:498
  117.9 2.0 %copy.6 = f32[2,64,32,256]{3,2,1,0:T(8,128)} copy(f32[2,64,32,256]{3,2,1,0:T(8,128)S(1)} %shard_map.46) | data formatting | bytes 8388608

commit v3 on v2

--- a/solution.py
+++ b/solution.py
@@ -47,9 +47,10 @@
 
 
 def kernel(cfg, hin, solid, rank, raw, out, f0, f1, tr, xh1, xh2, zh1, zh2, de1, de2,
-           mask, coef, sel, sel_t, lx, lr, rx, rr, table, lt, rt, raw_sem, loc_sem, swap_s, swap_r,
-           x1_s, x1_r, x2_s, x2_r, z1_s, z1_r, z2_s, z2_r, low_s, rate_s, meet_r, back_s, back_r, keep_sem):
-    planes, rows_y, rows_z, local, nc, nm, ns = cfg
+           mask, coef, sel, sel_t, lx, lr, table, lt, rt, raw_sem, loc_sem, swap_s, swap_r,
+           x1_s, x1_r, x2_s, x2_r, z1_s, z1_r, z2_s, z2_r, low_s, meet_r, back_s, back_r, keep_sem):
+    planes, rows_y, rows_z, local, nc, nm, spans = cfg
+    ns = len(spans)
     per = local // BLOCK
     levels = 2 * per
     half = rows_y // 2
@@ -249,31 +250,34 @@
 
         loop(0, ROWS, row)
 
+    def slot(j):
+        return pl.ds(pl.multiple_of(j * WIDE, WIDE), WIDE)
+
     def take_low(j):
-        total = jnp.zeros((cells, WIDE), jnp.float32)
-        for level in range(levels):
-            x = tr[level // per, :, rows2(j), :, lanes(level)].reshape(cells, BLOCK)
-            for term in split3(x):
-                total += dot(term, sel[level])
-        lx[j] = total
-
-    def owner(j):
-        return lax.rem(j, ns)
-
-    def distance(j):
-        return lax.rem(owner(j) + ns - q, ns)
-
-    def low_send(j):
-        return remote(lx.at[j], lr.at[j, distance(j) - 1], low_s, meet_r.at[j], (c, owner(j) * 2 + p))
-
-    def rate_send(j, d):
-        return remote(rx.at[j], rr.at[j], rate_s, meet_r.at[j], peer(d))
-
-    def collide(j):
-        low = lx[j]
-        for d in range(1, ns):
-            low = low + lr[j, d - 1]
-        lt[...] = low.T
+        total = jnp.zeros((3 * cells, WIDE), jnp.float32)
+        for blk in range(2):
+            x = tr[blk, :, rows2(j)].reshape(cells, local)
+            total += dot(jnp.concatenate(split3(x), axis=0), sel[blk])
+        total = total[0:cells] + total[cells : 2 * cells] + total[2 * cells : 3 * cells]
+        lx[slot(j), :] = total.T
+
+    def as_source(f):
+        for s, (lo, hi) in enumerate(spans):
+            pl.when(q == s)(functools.partial(f, s, lo, hi))
+
+    def low_send(j, s, o):
+        lo, hi = spans[s]
+        return remote(lx.at[pl.ds(pl.multiple_of(j * WIDE + lo, 8), hi - lo)], lr.at[j, s, pl.ds(0, hi - lo)], low_s, meet_r.at[j],
+                      (c, o * 2 + p))
+
+    def others(s):
+        return [o for o in range(ns) if o != s]
+
+    def collide(j, s, lo, hi):
+        lt[...] = lx[slot(j), :]
+        for o in others(s):
+            first_rank, last_rank = spans[o]
+            lt[first_rank:last_rank, :] += lr[j, o, 0 : last_rank - first_rank]
         rt[...] = jnp.zeros_like(rt)
 
         def step(start, count, columns):
@@ -282,7 +286,7 @@
             factors = jnp.concatenate(
                 [(rows[i : i + 1, :] * values) for i in range(count)], axis=0
             ).astype(jnp.bfloat16)
-            rt[0:BASIS_SIZE, :] += dot(table[:, columns], factors)
+            rt[lo:hi, :] += dot(table[lo:hi, columns], factors)
 
         def block(g):
             width = GROUP * BASIS_SIZE
@@ -293,13 +297,13 @@
         if groups * GROUP < BASIS_SIZE:
             step(groups * GROUP, BASIS_SIZE - groups * GROUP,
                  pl.ds(groups * GROUP * BASIS_SIZE, (BASIS_SIZE - groups * GROUP) * BASIS_SIZE))
-        rx[j] = rt[...].T
-
-    def lift(j, rates):
-        terms = split3(rates)
-        for level in range(levels):
-            add = sum(dot(term, sel_t[level]) for term in terms) * DTC
-            tr[level // per, :, rows2(j), :, lanes(level)] += add.reshape(planes, ROWS, rows_z, BLOCK)
+
+    def lift(j):
+        terms = jnp.concatenate(split3(rt[...].T), axis=0)
+        for blk in range(2):
+            add = dot(terms, sel_t[blk])
+            add = (add[0:cells] + add[cells : 2 * cells] + add[2 * cells : 3 * cells]) * DTC
+            tr[blk, :, rows2(j)] += add.reshape(planes, ROWS, rows_z, local)
 
     def give_back(j):
         return remote(tr.at[other, :, rows2(j)], out.at[:, pl.ds(p * half + j * ROWS, ROWS)],
@@ -360,8 +364,8 @@
         coef[4 + j : 5 + j] = low_root(0 * lane + level)
         coef[4 + levels + j : 5 + levels + j] = high_root(0 * lane + level, MA)
         mine = jnp.where(rank[pl.ds(level, 1), :] == wide, 1.0, 0.0)
-        sel_t[j] = mine.astype(jnp.bfloat16)
-        sel[j] = mine.T.astype(jnp.bfloat16)
+        sel_t[j // per, :, lanes(j)] = mine.astype(jnp.bfloat16)
+        sel[j // per, lanes(j), :] = mine.T.astype(jnp.bfloat16)
 
     clear = [jnp.where(solid[pln] != 0, 0.0, 1.0).astype(jnp.bfloat16) for pln in range(planes)]
     line = lax.broadcasted_iota(jnp.int32, (rows_y, BLOCK), 0)
@@ -413,31 +417,22 @@
             def _():
                 take_low(j)
 
-                @pl.when(q != owner(j))
-                def _():
-                    low_send(j).start()
+            as_source(lambda s, lo, hi: start_all(low_send(j, s, o) for o in others(s)))
 
             @pl.when(jnp.logical_not(is_source))
             def _():
                 finish(j)
 
         def meet(j):
-            @pl.when(jnp.logical_and(is_source, q == owner(j)))
-            def _():
+            def one(s, lo, hi):
                 if ns > 1:
-                    whole(lr.at[j], low_s, meet_r.at[j]).wait_recv()
-                collide(j)
-                for d in range(1, ns):
-                    rate_send(j, d).start()
-                lift(j, rx[j])
+                    rows = sum(spans[o][1] - spans[o][0] for o in others(s))
+                    whole(lx.at[pl.ds(0, rows)], low_s, meet_r.at[j]).wait_recv()
+                collide(j, s, lo, hi)
+                lift(j)
                 finish(j)
 
-        def settle(j):
-            @pl.when(jnp.logical_and(is_source, q != owner(j)))
-            def _():
-                whole(rr.at[j], rate_s, meet_r.at[j]).wait_recv()
-                lift(j, rr[j])
-                finish(j)
+            as_source(one)
 
         during(t, first, arrive)
         during(t - 2, first, slope1)
@@ -450,9 +445,8 @@
             raw_copy.wait()
 
         during(t - 8, chunks, meet)
-        during(t - 10, chunks, settle)
-
-    loop(0, chunks + 11, advance)
+
+    loop(0, chunks + 9, advance)
 
     whole(f0.at[p], swap_s, swap_s).wait_send()
     whole(xh1.at[:, :, pl.ds(1, first * ROWS)], x1_s, x1_s).wait_send()
@@ -460,11 +454,8 @@
     z_sent(de1, z1_s, pl.ds(1, first * ROWS))
     z_sent(de2, z2_s, pl.ds(2, half))
     if ns > 1:
-        @pl.when(is_source)
-        def _():
-            share = chunks // ns
-            whole(lx.at[pl.ds(0, chunks - share)], low_s, low_s).wait_send()
-            whole(lx.at[pl.ds(0, share * (ns - 1))], rate_s, rate_s).wait_send()
+        as_source(lambda s, lo, hi: whole(
+            lr.at[:, pl.ds(0, ns - 1), pl.ds(0, hi - lo)], low_s, low_s).wait_send())
 
     pltpu.make_async_copy(tr.at[p, :, pl.ds(2, half)], tr.at[p, :, pl.ds(2, half)], keep_sem).wait()
     whole(tr.at[other, :, pl.ds(2, half)], back_s, back_s).wait_send()
@@ -486,13 +477,14 @@
     flags = (index // BLOCK + index // MC % MB + index % MC <= LDEG).astype(np.int32)
     rank = jnp.asarray(np.where(flags == 1, np.cumsum(flags) - 1, -1).reshape(MA, BLOCK), jnp.int32)
 
-    peers = max(ns - 1, 1)
+    marks = [int(flags[: min(s * levels, MA) * BLOCK].sum()) for s in range(ns + 1)]
+    spans = [(lo // 16 * 16, min(-(-hi // 16) * 16, BASIS_SIZE)) for lo, hi in zip(marks[:-1], marks[1:])]
     cells = planes * ROWS * rows_z
     field = pltpu.VMEM((2, planes, ext, rows_z, local), jnp.float32)
     halo = pltpu.VMEM((2, 2, ext, rows_z, local), jnp.float32)
     slope = pltpu.VMEM((2, planes, ext, rows_z, BLOCK), jnp.float32)
     dma = pltpu.SemaphoreType.DMA
-    cfg = (planes, rows_y, rows_z, local, nc, nm, ns)
+    cfg = (planes, rows_y, rows_z, local, nc, nm, spans)
     vmem = pl.BlockSpec(memory_space=pltpu.VMEM)
     anywhere = pl.BlockSpec(memory_space=pl.ANY)
     return pl.pallas_call(
@@ -504,17 +496,15 @@
             field, field, field, halo, halo, slope, slope, slope, slope,
             pltpu.VMEM((planes, ext, rows_z, BLOCK), jnp.float32),
             pltpu.VMEM((4 + 2 * levels + -(4 + 2 * levels) % 8, BLOCK), jnp.float32),
-            pltpu.VMEM((levels, BLOCK, WIDE), jnp.bfloat16),
-            pltpu.VMEM((levels, WIDE, BLOCK), jnp.bfloat16),
-            pltpu.VMEM((chunks, cells, WIDE), jnp.float32),
-            pltpu.VMEM((chunks, peers, cells, WIDE), jnp.float32),
-            pltpu.VMEM((chunks, cells, WIDE), jnp.float32),
-            pltpu.VMEM((chunks, cells, WIDE), jnp.float32),
+            pltpu.VMEM((2, local, WIDE), jnp.bfloat16),
+            pltpu.VMEM((2, WIDE, local), jnp.bfloat16),
+            pltpu.VMEM((chunks * WIDE, cells), jnp.float32),
+            pltpu.VMEM((chunks, ns, max(hi - lo for lo, hi in spans), cells), jnp.float32),
             pltpu.VMEM((BASIS_SIZE, BASIS_SIZE * BASIS_SIZE), jnp.bfloat16),
             pltpu.VMEM((WIDE, cells), jnp.float32),
             pltpu.VMEM((WIDE, cells), jnp.float32),
             dma, dma, dma, dma((ext // ROWS,)), dma, dma((chunks + 1,)), dma, dma((chunks,)),
-            dma, dma((chunks + 1,)), dma, dma((chunks,)), dma, dma, dma((chunks,)), dma, dma, dma,
+            dma, dma((chunks + 1,)), dma, dma((chunks,)), dma, dma((chunks,)), dma, dma, dma,
         ],
         compiler_params=pltpu.CompilerParams(
             collective_id=0, has_side_effects=True, vmem_limit_bytes=54 * 1024 * 1024

time: 120 us -> 116 us (0.967)
  Pallas kernels: 118 us -> 114 us
    pallas_call x1, Pallas kernels: 118 us -> 114 us  [body(): pl.pallas_call(functools.partial(kernel, cfg), out_shape=pltpu.VMEM(hermi...]
where the time goes in v3:
time: 116 us
  Pallas kernels  114 us (98%)
  local copies, waits for them, and re-layouts  2.02 us (2%)
    pallas_call x1, Pallas kernels, body(): pl.pallas_call(functools.partial(kernel, cfg), out_shape=pltpu.VMEM(hermi...  114 us

profile of v3, /device:TPU:0, one launch (start us, length us, event | category | flops | bytes accessed | tf_op | source)
XLA Modules:
  0.0 116.1 jit_solution(3207557868212275998)
XLA Ops:
  0.0 114.1 %shard_map.46 = f32[2,64,32,256]{3,2,1,0:T(8,128)S(1)} custom-call(f32[2,64,32,256]{3,2,1,0:T(8,128)} %hin.1, s32[2,32,64]{2,1,0:T(8,128)} %bitcast.3, s32[16,128]{1,0:T(8,128)} %constant.2.clone.rank, bf16[120,14400]{1,0:T(8,128)(2,1)} %bitcast.2), custom_call_target="tpu_custom_call" | custom-call | tf_op jit(solution)/shard_map/pallas_call | solution.py:490
  114.1 2.0 %copy.6 = f32[2,64,32,256]{3,2,1,0:T(8,128)} copy(f32[2,64,32,256]{3,2,1,0:T(8,128)S(1)} %shard_map.46) | data formatting | bytes 8388608

commit v4 on v3

--- a/solution.py
+++ b/solution.py
@@ -19,7 +19,8 @@
 WIDE = 128
 GROUP = 64
 ROWS = 2
-LEAD = 5
+LEAD = 8
+EARLY = 6
 
 CFL = 0.04
 DTC = 0.2
@@ -48,7 +49,7 @@
 
 def kernel(cfg, hin, solid, rank, raw, out, f0, f1, tr, xh1, xh2, zh1, zh2, de1, de2,
            mask, coef, sel, sel_t, lx, lr, table, lt, rt, raw_sem, loc_sem, swap_s, swap_r,
-           x1_s, x1_r, x2_s, x2_r, z1_s, z1_r, z2_s, z2_r, low_s, meet_r, back_s, back_r, keep_sem):
+           x1_s, x1_r, x2_s, x2_r, x3_r, z1_s, z1_r, z2_s, z2_r, low_s, meet_r, brink_s, brink_r, back_s, back_r, keep_sem):
     planes, rows_y, rows_z, local, nc, nm, spans = cfg
     ns = len(spans)
     per = local // BLOCK
@@ -100,7 +101,7 @@
     def grid_row(side, e):
         return lax.rem(side * half + (rows_y - 2) + e, rows_y)
 
-    own_pieces = [(0, 2), (2, half + 2), (half + 2, ext)]
+    own_pieces = [(1, 2), (2, half + 2), (half + 2, half + 3)]
 
     def own(i):
         lo, hi = own_pieces[i]
@@ -122,36 +123,42 @@
             src_ref=src, dst_ref=dst, send_sem=s, recv_sem=r, device_id=dev, device_id_type=MESH
         )
 
-    arrivals = ext // ROWS
-    first = chunks + 1
-
-    def rows0(k):
-        return pl.ds(k * ROWS, ROWS)
-
-    def rows1(i):
-        return pl.ds(i * ROWS + 1, ROWS)
-
-    def rows2(j):
-        return pl.ds(j * ROWS + 2, ROWS)
-
-    def swap(k):
-        where = pl.ds(grid_row(other, k * ROWS), ROWS)
-        return remote(hin.at[:, where], f0.at[p, :, rows0(k)], swap_s, swap_r.at[k], mate)
-
-    def swap_in(k):
-        where = pl.ds(grid_row(other, k * ROWS), ROWS)
-        return remote(hin.at[:, where], f0.at[other, :, rows0(k)], swap_s, swap_r.at[k], mate)
-
-    def edge(field, halo, ss, rs, blk, k, where):
-        up = remote(field.at[blk, planes - 1, where], halo.at[0, blk, where], ss, rs.at[k], after)
-        down = remote(field.at[blk, 0, where], halo.at[1, blk, where], ss, rs.at[k], before)
+    brinks = (1, half + 2)
+
+    def pair(u):
+        return pl.ds(u * ROWS + 2, ROWS)
+
+    def turn(i):
+        return lax.rem(i + chunks - 1, chunks)
+
+    def late(k):
+        return k + lax.div(k, chunks - 2) * (2 * chunks - 3 - 2 * k)
+
+    def swap(u, who):
+        return remote(hin.at[:, pl.ds(grid_row(other, u * ROWS + 2), ROWS)], f0.at[who, :, pair(u)],
+                      swap_s, swap_r.at[u], mate)
+
+    def swap_brink(n, who):
+        return remote(hin.at[:, pl.ds(grid_row(other, brinks[n]), 1)], f0.at[who, :, pl.ds(brinks[n], 1)],
+                      swap_s, swap_r.at[chunks + n], mate)
+
+    def brink(n):
+        return remote(f1.at[:, :, pl.ds((half + 1, 2)[n], 1)], f1.at[:, :, pl.ds(brinks[n], 1)],
+                      brink_s, brink_r.at[n], mate)
+
+    def edge(field, halo, ss, rs, blk, k, where, span):
+        up = remote(field.at[blk, planes - 1, where, :, span], halo.at[0, blk, where, :, span], ss, rs.at[k], after)
+        down = remote(field.at[blk, 0, where, :, span], halo.at[1, blk, where, :, span], ss, rs.at[k], before)
         return up, down
 
-    def edge1(slot, i):
-        return edge(f0, xh1, x1_s, x1_r, (p, other)[slot], i, rows1(i))
-
-    def edge2(blk, j):
-        return edge(f1, xh2, x2_s, x2_r, blk, j, rows2(j))
+    def edge1(blk, u):
+        return edge(f0, xh1, x1_s, x1_r, blk, u, pair(u), pl.ds(0, local))
+
+    def edge2(blk, u):
+        return edge(f1, xh2, x2_s, x2_r, blk, u, pair(u), pl.ds((local - BLOCK) * blk, BLOCK))
+
+    def edge3(blk, u):
+        return edge(f1, xh2, x2_s, x3_r, blk, u, pair(u), pl.ds(BLOCK * (1 - blk), local - BLOCK))
 
     def whole(ref, s, r):
         return remote(ref, ref, s, r, mate)
@@ -212,11 +219,11 @@
         def _():
             whole(de.at[0, :, where], ss, ss).wait_send()
 
-    def z1(i):
-        return de1, zh1, z1_s, z1_r, i, rows1(i)
-
-    def z2(j):
-        return de2, zh2, z2_s, z2_r, j, rows2(j)
+    def z1(u):
+        return de1, zh1, z1_s, z1_r, u, pair(u)
+
+    def z2(u):
+        return de2, zh2, z2_s, z2_r, u, pair(u)
 
     wx = 0.5 * 2.0 * math.sqrt(MA)
     wy = 0.5 * 2.0 * math.sqrt(MB)
@@ -256,7 +263,7 @@
     def take_low(j):
         total = jnp.zeros((3 * cells, WIDE), jnp.float32)
         for blk in range(2):
-            x = tr[blk, :, rows2(j)].reshape(cells, local)
+            x = tr[blk, :, pair(j)].reshape(cells, local)
             total += dot(jnp.concatenate(split3(x), axis=0), sel[blk])
         total = total[0:cells] + total[cells : 2 * cells] + total[2 * cells : 3 * cells]
         lx[slot(j), :] = total.T
@@ -303,14 +310,14 @@
         for blk in range(2):
             add = dot(terms, sel_t[blk])
             add = (add[0:cells] + add[cells : 2 * cells] + add[2 * cells : 3 * cells]) * DTC
-            tr[blk, :, rows2(j)] += add.reshape(planes, ROWS, rows_z, local)
+            tr[blk, :, pair(j)] += add.reshape(planes, ROWS, rows_z, local)
 
     def give_back(j):
-        return remote(tr.at[other, :, rows2(j)], out.at[:, pl.ds(p * half + j * ROWS, ROWS)],
+        return remote(tr.at[other, :, pair(j)], out.at[:, pl.ds(p * half + j * ROWS, ROWS)],
                       back_s, back_r, mate)
 
     def keep(j):
-        return pltpu.make_async_copy(tr.at[p, :, rows2(j)], out.at[:, pl.ds(p * half + j * ROWS, ROWS)],
+        return pltpu.make_async_copy(tr.at[p, :, pair(j)], out.at[:, pl.ds(p * half + j * ROWS, ROWS)],
                                      keep_sem)
 
     def finish(j):
@@ -326,10 +333,15 @@
         def _():
             f(index)
 
-    loop(0, 2, lambda k: swap(k).start())
-    pltpu.make_async_copy(f0.at[p], f0.at[p], loc_sem).wait()
-    loop(0, min(LEAD, first), lambda i: start_all(edge1(0, i)))
-    loop(2, arrivals, lambda k: swap(k).start())
+    swap(chunks - 1, p).start()
+    near = pl.ds(1, half + 2)
+    pltpu.make_async_copy(f0.at[p, :, near], f0.at[p, :, near], loc_sem).wait()
+    loop(0, min(LEAD, chunks), lambda i: start_all(edge1(p, turn(i))))
+    swap(chunks - 2, p).start()
+    for n in (1, 0):
+        swap_brink(n, p).start()
+    early = min(EARLY, chunks - 2)
+    loop(0, early, lambda u: swap(u, p).start())
 
     @pl.when(is_source)
     def _():
@@ -375,55 +387,82 @@
         for pln in range(planes):
             mask[pln, e] = dot(clear[pln], pick) * CFL
 
-    loop(1, ext - 1, spread)
+    loop(2, half + 2, spread)
 
     def advance(t):
         def arrive(i):
-            @pl.when(i == 0)
+            u = turn(i)
+
+            @pl.when(i == 1)
             def _():
-                swap_in(0).wait_recv()
-
-            swap_in(i + 1).wait_recv()
-            start_all(edge1(1, i))
-
-            @pl.when(i + LEAD < first)
+                swap(chunks - 2, other).wait_recv()
+                for n in (1, 0):
+                    swap_brink(n, other).wait_recv()
+
+            @pl.when(i < chunks - 1)
             def _():
-                start_all(edge1(0, i + LEAD))
+                swap(u, other).wait_recv()
+
+            start_all(edge1(other, u))
+
+            @pl.when(i + LEAD < chunks)
+            def _():
+                start_all(edge1(p, turn(i + LEAD)))
 
         def slope1(i):
-            whole(xh1.at[:, :, rows1(i)], x1_s, x1_r.at[i]).wait_recv()
-            slopes(f0, xh1, de1, i * ROWS + 1)
-            z_start(*z1(i))
-
-        def slope2(j):
-            whole(xh2.at[:, :, rows2(j)], x2_s, x2_r.at[j]).wait_recv()
-            slopes(f1, xh2, de2, j * ROWS + 2)
-            z_start(*z2(j))
+            u = turn(i)
+            whole(xh1.at[:, :, pair(u)], x1_s, x1_r.at[u]).wait_recv()
+            slopes(f0, xh1, de1, u * ROWS + 2)
+            z_start(*z1(u))
+
+        def slope2(k):
+            u = late(k)
+            whole(xh2.at[:, :, pair(u), :, pl.ds(0, BLOCK)], x2_s, x2_r.at[u]).wait_recv()
+            slopes(f1, xh2, de2, u * ROWS + 2)
+            z_start(*z2(u))
 
         def move1(i):
-            z_arrived(*z1(i))
-            substep(f0, xh1, zh1, f1, i * ROWS + 1)
-
-            @pl.when(i >= 1)
-            def _():
+            u = turn(i)
+            z_arrived(*z1(u))
+            substep(f0, xh1, zh1, f1, u * ROWS + 2)
+            for n in range(2):
+                @pl.when(i == n)
+                def _(n=n):
+                    brink(n).start()
+                    if n == 1:
+                        loop(early, chunks - 2, lambda u: swap(u, p).start())
+
+            for blk in range(2):
+                start_all(edge2(blk, u))
+            if per > 1:
                 for blk in range(2):
-                    start_all(edge2(blk, i - 1))
-
-        def move2(j):
-            z_arrived(*z2(j))
-            substep(f1, xh2, zh2, tr, j * ROWS + 2)
+                    start_all(edge3(blk, u))
+
+        def move2(k):
+            u = late(k)
+            for n, turn_of in enumerate((0, chunks - 2)):
+                @pl.when(k == turn_of)
+                def _(n=n):
+                    brink(n).wait_recv()
+
+            if per > 1:
+                whole(xh2.at[:, :, pair(u), :, pl.ds(BLOCK, local - BLOCK)], x2_s, x3_r.at[u]).wait_recv()
+            z_arrived(*z2(u))
+            substep(f1, xh2, zh2, tr, u * ROWS + 2)
 
             @pl.when(is_source)
             def _():
-                take_low(j)
-
-            as_source(lambda s, lo, hi: start_all(low_send(j, s, o) for o in others(s)))
+                take_low(u)
+
+            as_source(lambda s, lo, hi: start_all(low_send(u, s, o) for o in others(s)))
 
             @pl.when(jnp.logical_not(is_source))
             def _():
-                finish(j)
-
-        def meet(j):
+                finish(u)
+
+        def meet(k):
+            j = late(k)
+
             def one(s, lo, hi):
                 if ns > 1:
                     rows = sum(spans[o][1] - spans[o][0] for o in others(s))
@@ -434,24 +473,24 @@
 
             as_source(one)
 
-        during(t, first, arrive)
-        during(t - 2, first, slope1)
-        during(t - 6, chunks, slope2)
-        during(t - 3, first, move1)
-        during(t - 7, chunks, move2)
-
-        @pl.when(jnp.logical_and(is_source, t == 8))
+        during(t, chunks, arrive)
+        during(t - 1, chunks, slope1)
+        during(t - 2, chunks, move1)
+        during(t - 4, chunks, slope2)
+        during(t - 5, chunks, move2)
+        @pl.when(jnp.logical_and(is_source, t == 6))
         def _():
             raw_copy.wait()
 
-        during(t - 8, chunks, meet)
-
-    loop(0, chunks + 9, advance)
-
-    whole(f0.at[p], swap_s, swap_s).wait_send()
-    whole(xh1.at[:, :, pl.ds(1, first * ROWS)], x1_s, x1_s).wait_send()
+        during(t - 6, chunks, meet)
+
+    loop(0, chunks + 6, advance)
+
+    whole(f0.at[p, :, near], swap_s, swap_s).wait_send()
+    whole(xh1.at[:, :, pl.ds(2, half)], x1_s, x1_s).wait_send()
+    whole(f1.at[:, :, pl.ds(2, 2)], brink_s, brink_s).wait_send()
     whole(xh2.at[:, :, pl.ds(2, half)], x2_s, x2_s).wait_send()
-    z_sent(de1, z1_s, pl.ds(1, first * ROWS))
+    z_sent(de1, z1_s, pl.ds(2, half))
     z_sent(de2, z2_s, pl.ds(2, half))
     if ns > 1:
         as_source(lambda s, lo, hi: whole(
@@ -503,8 +542,8 @@
             pltpu.VMEM((BASIS_SIZE, BASIS_SIZE * BASIS_SIZE), jnp.bfloat16),
             pltpu.VMEM((WIDE, cells), jnp.float32),
             pltpu.VMEM((WIDE, cells), jnp.float32),
-            dma, dma, dma, dma((ext // ROWS,)), dma, dma((chunks + 1,)), dma, dma((chunks,)),
-            dma, dma((chunks + 1,)), dma, dma((chunks,)), dma, dma((chunks,)), dma, dma, dma,
+            dma, dma, dma, dma((chunks + 2,)), dma, dma((chunks,)), dma, dma((chunks,)), dma((chunks,)),
+            dma, dma((chunks,)), dma, dma((chunks,)), dma, dma((chunks,)), dma, dma((2,)), dma, dma, dma,
         ],
         compiler_params=pltpu.CompilerParams(
             collective_id=0, has_side_effects=True, vmem_limit_bytes=54 * 1024 * 1024

time: 116 us -> 115 us (level)
    pallas_call x1, Pallas kernels: 114 us -> 113 us  [body(): pl.pallas_call(functools.partial(kernel, cfg), out_shape=pltpu.VMEM(hermi...]
where the time goes in v4:
time: 115 us
  Pallas kernels  113 us (98%)
  local copies, waits for them, and re-layouts  2.02 us (2%)
    pallas_call x1, Pallas kernels, body(): pl.pallas_call(functools.partial(kernel, cfg), out_shape=pltpu.VMEM(hermi...  113 us

profile of v4, /device:TPU:0, one launch (start us, length us, event | category | flops | bytes accessed | tf_op | source)
XLA Modules:
  0.0 114.9 jit_solution(18329310218816178950)
XLA Ops:
  0.0 112.8 %shard_map.46 = f32[2,64,32,256]{3,2,1,0:T(8,128)S(1)} custom-call(f32[2,64,32,256]{3,2,1,0:T(8,128)} %hin.1, s32[2,32,64]{2,1,0:T(8,128)} %bitcast.3, s32[16,128]{1,0:T(8,128)} %constant.2.clone.rank, bf16[120,14400]{1,0:T(8,128)(2,1)} %bitcast.2), custom_call_target="tpu_custom_call" | custom-call | tf_op jit(solution)/shard_map/pallas_call | solution.py:529
  112.9 2.0 %copy.6 = f32[2,64,32,256]{3,2,1,0:T(8,128)} copy(f32[2,64,32,256]{3,2,1,0:T(8,128)S(1)} %shard_map.46) | data formatting | bytes 8388608

commit v5 on v4

--- a/solution.py
+++ b/solution.py
@@ -20,6 +20,7 @@
 GROUP = 64
 ROWS = 2
 LEAD = 8
+RING = 8
 EARLY = 6
 
 CFL = 0.04
@@ -134,6 +135,12 @@
     def late(k):
         return k + lax.div(k, chunks - 2) * (2 * chunks - 3 - 2 * k)
 
+    def ring(u):
+        return lax.rem(u, RING)
+
+    def ring2(u):
+        return lax.rem(u, RING) + lax.div(u, chunks - 1) * (RING - (chunks - 1) % RING)
+
     def swap(u, who):
         return remote(hin.at[:, pl.ds(grid_row(other, u * ROWS + 2), ROWS)], f0.at[who, :, pair(u)],
                       swap_s, swap_r.at[u], mate)
@@ -155,10 +162,10 @@
         return edge(f0, xh1, x1_s, x1_r, blk, u, pair(u), pl.ds(0, local))
 
     def edge2(blk, u):
-        return edge(f1, xh2, x2_s, x2_r, blk, u, pair(u), pl.ds((local - BLOCK) * blk, BLOCK))
+        return edge(f1, xh2, x2_s, x2_r, blk, ring2(u), pair(u), pl.ds((local - BLOCK) * blk, BLOCK))
 
     def edge3(blk, u):
-        return edge(f1, xh2, x2_s, x3_r, blk, u, pair(u), pl.ds(BLOCK * (1 - blk), local - BLOCK))
+        return edge(f1, xh2, x2_s, x3_r, blk, ring2(u), pair(u), pl.ds(BLOCK * (1 - blk), local - BLOCK))
 
     def whole(ref, s, r):
         return remote(ref, ref, s, r, mate)
@@ -220,10 +227,10 @@
             whole(de.at[0, :, where], ss, ss).wait_send()
 
     def z1(u):
-        return de1, zh1, z1_s, z1_r, u, pair(u)
+        return de1, zh1, z1_s, z1_r, ring(u), pair(u)
 
     def z2(u):
-        return de2, zh2, z2_s, z2_r, u, pair(u)
+        return de2, zh2, z2_s, z2_r, ring(u), pair(u)
 
     wx = 0.5 * 2.0 * math.sqrt(MA)
     wy = 0.5 * 2.0 * math.sqrt(MB)
@@ -274,7 +281,7 @@
 
     def low_send(j, s, o):
         lo, hi = spans[s]
-        return remote(lx.at[pl.ds(pl.multiple_of(j * WIDE + lo, 8), hi - lo)], lr.at[j, s, pl.ds(0, hi - lo)], low_s, meet_r.at[j],
+        return remote(lx.at[pl.ds(pl.multiple_of(j * WIDE + lo, 8), hi - lo)], lr.at[j, s, pl.ds(0, hi - lo)], low_s, meet_r.at[ring(j)],
                       (c, o * 2 + p))
 
     def others(s):
@@ -306,10 +313,10 @@
                  pl.ds(groups * GROUP * BASIS_SIZE, (BASIS_SIZE - groups * GROUP) * BASIS_SIZE))
 
     def lift(j):
-        terms = jnp.concatenate(split3(rt[...].T), axis=0)
+        terms = jnp.concatenate(split3(rt[...].T)[:2], axis=0)
         for blk in range(2):
             add = dot(terms, sel_t[blk])
-            add = (add[0:cells] + add[cells : 2 * cells] + add[2 * cells : 3 * cells]) * DTC
+            add = (add[0:cells] + add[cells : 2 * cells]) * DTC
             tr[blk, :, pair(j)] += add.reshape(planes, ROWS, rows_z, local)
 
     def give_back(j):
@@ -417,7 +424,7 @@
 
         def slope2(k):
             u = late(k)
-            whole(xh2.at[:, :, pair(u), :, pl.ds(0, BLOCK)], x2_s, x2_r.at[u]).wait_recv()
+            whole(xh2.at[:, :, pair(u), :, pl.ds(0, BLOCK)], x2_s, x2_r.at[ring2(u)]).wait_recv()
             slopes(f1, xh2, de2, u * ROWS + 2)
             z_start(*z2(u))
 
@@ -446,7 +453,7 @@
                     brink(n).wait_recv()
 
             if per > 1:
-                whole(xh2.at[:, :, pair(u), :, pl.ds(BLOCK, local - BLOCK)], x2_s, x3_r.at[u]).wait_recv()
+                whole(xh2.at[:, :, pair(u), :, pl.ds(BLOCK, local - BLOCK)], x2_s, x3_r.at[ring2(u)]).wait_recv()
             z_arrived(*z2(u))
             substep(f1, xh2, zh2, tr, u * ROWS + 2)
 
@@ -466,7 +473,7 @@
             def one(s, lo, hi):
                 if ns > 1:
                     rows = sum(spans[o][1] - spans[o][0] for o in others(s))
-                    whole(lx.at[pl.ds(0, rows)], low_s, meet_r.at[j]).wait_recv()
+                    whole(lx.at[pl.ds(0, rows)], low_s, meet_r.at[ring(j)]).wait_recv()
                 collide(j, s, lo, hi)
                 lift(j)
                 finish(j)
@@ -542,8 +549,8 @@
             pltpu.VMEM((BASIS_SIZE, BASIS_SIZE * BASIS_SIZE), jnp.bfloat16),
             pltpu.VMEM((WIDE, cells), jnp.float32),
             pltpu.VMEM((WIDE, cells), jnp.float32),
-            dma, dma, dma, dma((chunks + 2,)), dma, dma((chunks,)), dma, dma((chunks,)), dma((chunks,)),
-            dma, dma((chunks,)), dma, dma((chunks,)), dma, dma((chunks,)), dma, dma((2,)), dma, dma, dma,
+            dma, dma, dma, dma((chunks + 2,)), dma, dma((chunks,)), dma, dma((RING + 1,)), dma((RING + 1,)),
+            dma, dma((RING,)), dma, dma((RING,)), dma, dma((RING,)), dma, dma((2,)), dma, dma, dma,
         ],
         compiler_params=pltpu.CompilerParams(
             collective_id=0, has_side_effects=True, vmem_limit_bytes=54 * 1024 * 1024

time: 115 us -> 115 us (level)
  no operation moved by 1% of the time
where the time goes in v5:
time: 115 us; the launch traced here: 114 us
  Pallas kernels  112 us (97%)
  local copies, waits for them, and re-layouts  2.02 us (2%)
    pallas_call x1, Pallas kernels, body(): pl.pallas_call(functools.partial(kernel, cfg), out_shape=pltpu.VMEM(hermi...  112 us

profile of v5, /device:TPU:0, one launch (start us, length us, event | category | flops | bytes accessed | tf_op | source)
XLA Modules:
  0.0 114.5 jit_solution(1831104991352557137)
XLA Ops:
  0.0 112.4 %shard_map.46 = f32[2,64,32,256]{3,2,1,0:T(8,128)S(1)} custom-call(f32[2,64,32,256]{3,2,1,0:T(8,128)} %hin.1, s32[2,32,64]{2,1,0:T(8,128)} %bitcast.3, s32[16,128]{1,0:T(8,128)} %constant.2.clone.rank, bf16[120,14400]{1,0:T(8,128)(2,1)} %bitcast.2), custom_call_target="tpu_custom_call" | custom-call | tf_op jit(solution)/shard_map/pallas_call | solution.py:536
  112.4 2.0 %copy.6 = f32[2,64,32,256]{3,2,1,0:T(8,128)} copy(f32[2,64,32,256]{3,2,1,0:T(8,128)S(1)} %shard_map.46) | data formatting | bytes 8388608

commit v6 on v5

--- a/solution.py
+++ b/solution.py
@@ -524,7 +524,7 @@
     rank = jnp.asarray(np.where(flags == 1, np.cumsum(flags) - 1, -1).reshape(MA, BLOCK), jnp.int32)
 
     marks = [int(flags[: min(s * levels, MA) * BLOCK].sum()) for s in range(ns + 1)]
-    spans = [(lo // 16 * 16, min(-(-hi // 16) * 16, BASIS_SIZE)) for lo, hi in zip(marks[:-1], marks[1:])]
+    spans = [(lo // 16 * 16, min(-(-hi // 8) * 8, BASIS_SIZE)) for lo, hi in zip(marks[:-1], marks[1:])]
     cells = planes * ROWS * rows_z
     field = pltpu.VMEM((2, planes, ext, rows_z, local), jnp.float32)
     halo = pltpu.VMEM((2, 2, ext, rows_z, local), jnp.float32)

time: 115 us -> 115 us (level)
  no operation moved by 1% of the time
where the time goes in v6:
time: 115 us; the launch traced here: 114 us
  Pallas kernels  112 us (97%)
  local copies, waits for them, and re-layouts  2.02 us (2%)
    pallas_call x1, Pallas kernels, body(): pl.pallas_call(functools.partial(kernel, cfg), out_shape=pltpu.VMEM(hermi...  112 us

profile of v6, /device:TPU:0, one launch (start us, length us, event | category | flops | bytes accessed | tf_op | source)
XLA Modules:
  0.0 114.5 jit_solution(9975346888185978513)
XLA Ops:
  0.0 112.4 %shard_map.46 = f32[2,64,32,256]{3,2,1,0:T(8,128)S(1)} custom-call(f32[2,64,32,256]{3,2,1,0:T(8,128)} %hin.1, s32[2,32,64]{2,1,0:T(8,128)} %bitcast.3, s32[16,128]{1,0:T(8,128)} %constant.2.clone.rank, bf16[120,14400]{1,0:T(8,128)(2,1)} %bitcast.2), custom_call_target="tpu_custom_call" | custom-call | tf_op jit(solution)/shard_map/pallas_call | solution.py:536
  112.4 2.0 %copy.6 = f32[2,64,32,256]{3,2,1,0:T(8,128)} copy(f32[2,64,32,256]{3,2,1,0:T(8,128)S(1)} %shard_map.46) | data formatting | bytes 8388608
